TPU v7x, 32 devices: a whole 2x2x4 slice. The times are simulated.
32 devices in a mesh: kv: 4 (over y, x), seq: 8 (over z, core).
Axes of the slice: x: 2, y: 2, z: 4, core: 2. Of those that a mesh axis runs over, the one named last changes fastest.
Arguments:
- sampled_rows: int32 [768], replicated, may hold values from 0 to 2047, as said below
- query_vectors: bfloat16 [768, 64, 128], P('seq', 'kv'), may hold values from -150 to 150
- key_vectors: bfloat16 [2048, 8, 128], P('seq', 'kv'), may hold values from -6 to 6
Outputs:
- heavy_hitters: float32 [2048], P('seq')
Inputs may be any that keep to these rules, and one draw needn't show every extreme that they name: `sampled_rows`: strictly increasing sequence positions.
All inputs are finite; a program needn't handle non-finite values.
Results may differ from a plain program's by a relative error of at most 0.0003.
Values may be sent and summed in bfloat16 or wider, within the bound.
No kernel may reach another device: no remote copies, remote signals or barrier semaphores. Data moves between devices by JAX's collectives and lax.ppermute only.
A program may use at most 64 MiB of HBM per device.

v0:
```python
import math
import jax
import jax.numpy as jnp
from jax import lax
from jax.sharding import PartitionSpec as P

HD = 128
NEG = -1e30


def block_scores(query_block, key_block, factor):
    return (
        jnp.einsum("rgid,kgd->rgik", query_block, key_block, preferred_element_type=jnp.float32)
        * factor
    )


def visibility(rows_block, offset, amount):
    places = offset + jnp.arange(amount, dtype=jnp.int32)
    return places[None, None, None, :] <= rows_block[:, None, None, None]


def stats_block(query_block, rows_block, key_block, offset, running, factor):
    row_max, row_total = running
    scores = block_scores(query_block, key_block, factor)
    visible = visibility(rows_block, offset, key_block.shape[0])
    scores = jnp.where(visible, scores, NEG)
    new_max = jnp.maximum(row_max, jnp.max(scores, axis=-1))
    terms = jnp.where(visible, jnp.exp(scores - new_max[..., None]), 0.0)
    return (new_max, row_total * jnp.exp(row_max - new_max) + jnp.sum(terms, axis=-1))


def prob_columns(query_block, rows_block, key_block, offset, log_total, factor):
    scores = block_scores(query_block, key_block, factor)
    visible = visibility(rows_block, offset, key_block.shape[0])
    probability = jnp.where(visible, jnp.exp(scores - log_total[..., None]), 0.0)
    return jnp.sum(probability, axis=(0, 1, 2))


def on_device(sampled_rows, query_vectors, key_vectors):
    local_rows = query_vectors.shape[0]
    local_keys = key_vectors.shape[0]
    local_groups = key_vectors.shape[1]
    group_size = query_vectors.shape[1] // local_groups
    factor = 1.0 / math.sqrt(HD)
    seq_index = lax.axis_index("seq")
    grouped = query_vectors.reshape(local_rows, local_groups, group_size, HD)
    own_rows = lax.dynamic_slice_in_dim(sampled_rows, seq_index * local_rows, local_rows, 0)
    highest = jnp.max(own_rows)
    gathered = lax.all_gather(key_vectors, "seq", axis=0, tiled=True)
    total_keys = gathered.shape[0]
    key_stride = math.gcd(total_keys, 2048)

    def sweep(running, key_index):
        offset = key_index * key_stride

        def sweep_active(state):
            key_block = lax.dynamic_slice_in_dim(gathered, offset, key_stride, 0)
            return stats_block(grouped, own_rows, key_block, offset, state, factor)

        return (lax.cond(offset <= highest, sweep_active, lambda state: state, running), None)

    initial = (
        jnp.full((local_rows, local_groups, group_size), NEG, jnp.float32),
        jnp.zeros((local_rows, local_groups, group_size), jnp.float32),
    )
    (row_max, row_total), _ = lax.scan(
        sweep, initial, jnp.arange(total_keys // key_stride, dtype=jnp.int32)
    )
    log_total = row_max + jnp.log(row_total)

    def terms(offset, amount):
        stride = math.gcd(amount, 2048)

        def portion(block_index):
            first = block_index * stride

            def portion_active():
                key_block = lax.dynamic_slice_in_dim(gathered, first, stride, 0)
                return prob_columns(grouped, own_rows, key_block, first, log_total, factor)

            return lax.cond(
                first <= highest, portion_active, lambda: jnp.zeros((stride,), jnp.float32)
            )

        return lax.map(portion, jnp.arange(amount // stride, dtype=jnp.int32)).reshape(amount)

    columns = lax.psum_scatter(
        terms(jnp.int32(0), lax.axis_size("seq") * local_keys),
        "seq",
        scatter_dimension=0,
        tiled=True,
    )
    summed = lax.psum(columns, "kv")
    return summed * (1.0 / group_size)


def solution(mesh):
    placed = (P(), P("seq", "kv", None), P("seq", "kv", None))
    return jax.shard_map(on_device, mesh=mesh, in_specs=placed, out_specs=P("seq"), check_vma=False)
```

profile of v0, /device:TPU:0, one launch (start us, length us, event | category | flops | bytes accessed | tf_op | source)
XLA Modules:
  0.0 79.1 jit_solution(16837584428170734171)
XLA Ops:
  6.5 0.0 all-gather.2.cloned.1.call-start
  6.5 1.6 %copy.6 = bf16[256,2,128]{2,0,1:T(8,128)(2,1)} copy(bf16[256,2,128]{2,1,0:T(2,128)(2,1)} %param.9) | data formatting | bytes 262144 | tf_op args[2]
  8.1 0.0 all-gather.2.cloned.1.call-update
  8.1 1.4 %fusion.7 = (s32[]{:T(128)}, s32[96]{0:T(128)S(1)}) fusion(s32[768]{0:T(1024)} %param.7, s32[]{:T(128)S(6)} %select_n.15), kind=kLoop, calls=%fused_computation.14 | loop fusion | flops 95 | bytes 776 | tf_op jit(solution)/shard_map/reduce_max | solution.py:49
  10.2 1.1 %copy.7 = bf16[96,16,128]{2,0,1:T(8,128)(2,1)S(1)} copy(bf16[96,16,128]{2,1,0:T(8,128)(2,1)} %param.8) | data formatting | bytes 786432 | tf_op args[1]
  11.3 1.3 %dynamic-slice = u32[1]{0:T(128)} dynamic-slice(u32[32]{0:T(128)} %constant.61, u32[]{:T(128)S(6)} %add.42), dynamic_slice_sizes={1} | dynamic-slice | bytes 12
  13.3 20.7 %all-gather.2.cloned.1.call-done = bf16[2048,2,128]{2,0,1:T(8,128)(2,1)} async-done(((bf16[256,2,128]{2,0,1:T(8,128)(2,1)}), bf16[2048,2,128]{2,0,1:T(8,128)(2,1)}) %all-gather.2.cloned.1.call-update) | async-done | bytes 1048592 | tf_op jit(solution)/shard_map/all_gather | solution.py:50
  33.9 7.3 %conditional.2 = ((f32[96,2,8]{0,2,1:T(8,128)S(1)}, f32[96,2,8]{0,2,1:T(8,128)S(1)})) conditional(s32[]{:T(128)} %convert_element_type.6, (f32[96,2,8]{0,2,1:T(8,128)S(1)}, f32[96,2,8]{0,2,1:T(8,128)S(1)}) %tuple.33, (s32[96]{0:T(128)S(1)}, bf16[2048,2,128]{2,0,1:T(8,128)(2,1)}, bf16[96,2,8,128]{3,0,2,1:T(8,128)(2,1)S(1)}, f32[96,2,8]{0,2,1:T(8,128)S(1)}, ...), branch_computations={%region_1.2_spmd, %region_2.5_spmd} | conditional | flops 830671872 | bytes 27277720 | solution.py:61
  33.9 0.2 iota_compare_fusion
  34.1 3.6 %fusion = (f32[96,2,8]{0,2,1:T(8,128)S(1)}, f32[2,2048,96,8]{1,2,3,0:T(8,128)S(1)}) fusion(pred[96,2048]{1,0:T(8,128)(4,1)S(1)} %iota_compare_fusion, bf16[96,2,8,128]{3,0,2,1:T(8,128)(2,1)S(1)} %get-tuple-element.91, bf16[2048,2,128]{2,0,1:T(8,128)(2,1)} %get-tuple-element.90), kind=kOutput, calls=%fused_computation.2 | convolution fusion | flops 814742016 | bytes 14227456 | tf_op jit(solution)/shard_map/while/body/eval_jaxpr/cond/branch_1_fun/rgid,kgd->rgik/dot_general | solution.py:13
  37.7 3.5 %select_reduce_fusion = f32[96,2,8]{0,2,1:T(8,128)S(1)} fusion(f32[2,2048,96,8]{1,2,3,0:T(8,128)S(1)} %get-tuple-element.110, f32[96,2,8]{0,2,1:T(8,128)S(1)} %max.2, pred[96,2048]{1,0:T(8,128)(4,1)S(1)} %iota_compare_fusion), kind=kLoop, calls=%fused_computation.1 | loop fusion | flops 15727104 | bytes 12791808 | tf_op jit(solution)/shard_map/while/body/eval_jaxpr/cond/branch_1_fun/reduce_sum | solution.py:30
  41.3 4.9 %conditional.3 = (f32[2048]{0:T(1024)S(1)}) conditional(s32[]{:T(128)} %convert_element_type.6, () %tuple.32, (s32[96]{0:T(128)S(1)}, bf16[2048,2,128]{2,0,1:T(8,128)(2,1)}, bf16[96,2,8,128]{3,0,2,1:T(8,128)(2,1)S(1)}, f32[96,2,8]{0,2,1:T(8,128)S(1)}, f32[96,2,8]{0,2,1:T(8,128)S(1)}) %tuple.52), branch_computations={%region_5.0_spmd, %region_6.8_spmd} | conditional | flops 818085376 | bytes 1868168 | solution.py:82
  41.3 0.2 iota_compare_fusion.1
  41.5 4.7 %fusion.5 = f32[2048]{0:T(1024)S(1)} fusion(f32[96,2,8]{0,2,1:T(8,128)S(1)} %add.38, pred[96,2048]{1,0:T(8,128)(4,1)S(1)} %iota_compare_fusion.1, bf16[96,2,8,128]{3,0,2,1:T(8,128)(2,1)S(1)} %get-tuple-element.95, bf16[2048,2,128]{2,0,1:T(8,128)(2,1)} %get-tuple-element.94), kind=kOutput, calls=%fused_computation.10 | convolution fusion | flops 817887232 | bytes 1652736 | tf_op jit(solution)/shard_map/while/body/eval_jaxpr/cond/branch_1_fun/rgid,kgd->rgik/dot_general | solution.py:13
  46.1 15.8 %all-reduce = f32[2048]{0:T(1024)S(1)} all-reduce(f32[2048]{0:T(1024)S(1)} %get-tuple-element.116), channel_id=2, replica_groups=mesh['kv'=4,'seq'=8] {'seq'}, use_global_device_ids=true, to_apply=%region_8.9.clone | all-reduce | flops 2048 | bytes 16384
  61.9 0.1 dynamic-slice.1
  62.0 9.7 %psum.7 = f32[256]{0:T(256)S(1)} all-reduce(f32[256]{0:T(256)S(1)} %dynamic-slice.1), channel_id=1, replica_groups=mesh['kv'=4,'seq'=8] {'kv'}, use_global_device_ids=true, to_apply=%region_9.10 | all-reduce | flops 256 | bytes 2048 | tf_op jit(solution)/shard_map/psum | solution.py:94
  71.7 0.6 broadcast_multiply_fusion
  (7 shorter events, 0.0 us)
Async XLA Ops:
  6.5 27.4 %all-gather.2.cloned.1.call-start = ((), (), s32[]{:S(2)}) async-start(), calls=%async_computation | async-start | bytes 1179648 | tf_op jit(solution)/shard_map/all_gather | solution.py:50
Sparse Core Ops, SparseCore 0:
  8.9 24.9 all-gather.1
where the time goes:
time: 79.4 us; the launch traced here: 79.1 us
  blocking collectives  25.4 us (32%)
  waiting for transfers between devices  20.7 us (26%)
  between operations  14.7 us (19%)
  matrix products  8.2 us (10%)
  other arithmetic  5.88 us (7%)
  local copies, waits for them, and re-layouts  4.06 us (5%)
    all_gather x1, waiting for transfers between devices, on_device(): gathered = lax.all_gather(key_vectors, 'seq', axis=0, tiled=True)  20.7 us
    unnamed x1, blocking collectives  15.8 us
    psum x1, blocking collectives, on_device(): summed = lax.psum(columns, 'kv')  9.67 us
    dot_general x2, matrix products, block_scores(): jnp.einsum('rgid,kgd->rgik', query_block, key_block, preferred_element_ty...  8.2 us
    unnamed x4, local copies, waits for them, and re-layouts  4.05 us
    reduce_sum x1, other arithmetic, stats_block(): jnp.sum(terms, axis=-1)  3.55 us
  transfers between devices with their start and end apart: 1, of which 1 were waited for; matrix products, arithmetic and copies ran while one was open for 5% of the time, Pallas kernels for 0%

commit v1 on v0

--- a/solution.py
+++ b/solution.py
@@ -47,7 +47,12 @@
     grouped = query_vectors.reshape(local_rows, local_groups, group_size, HD)
     own_rows = lax.dynamic_slice_in_dim(sampled_rows, seq_index * local_rows, local_rows, 0)
     highest = jnp.max(own_rows)
-    gathered = lax.all_gather(key_vectors, "seq", axis=0, tiled=True)
+    ring = [key_vectors]
+    for hop in range(7):
+        ring.append(lax.ppermute(ring[-1], "seq", [(dev, (dev + 1) % 8) for dev in range(8)]))
+    gathered = jnp.roll(
+        jnp.concatenate(ring[::-1], axis=0), (lax.axis_index("seq") + 1) * ring[0].shape[0], axis=0
+    )
     total_keys = gathered.shape[0]
     key_stride = math.gcd(total_keys, 2048)
 

time: 79.4 us -> 83.5 us (1.052)
  waiting for transfers between devices: 20.7 us -> 38.6 us
  between operations: 14.7 us -> 1.55 us
  matrix products: 8.2 us -> 5.79 us
  blocking collectives: 25.4 us -> 26.8 us
    ppermute x0 -> x7, waiting for transfers between devices: none -> 38.6 us  [on_device(): lax.ppermute(ring[-1], 'seq', [(dev, (dev + 1) % 8) for dev in range(8)])]
    all_gather x1 -> x0, waiting for transfers between devices: 20.7 us -> none  [on_device(): gathered = lax.all_gather(key_vectors, 'seq', axis=0, tiled=True)]
    dot_general x2, matrix products: 8.2 us -> 5.79 us  [block_scores(): jnp.einsum('rgid,kgd->rgik', query_block, key_block, preferred_element_ty...]
    unnamed x4 -> x21, local copies, waits for them, and re-layouts: 4.05 us -> 3.82 us
  transfers between devices with their start and end apart: 1 -> 7, of which waited for: 1 -> 7; matrix products, arithmetic and copies ran while one was open for 5% -> 5% of each run, Pallas kernels for 0% -> 0%
where the time goes in v1:
time: 83.5 us; the launch traced here: 83.2 us
  waiting for transfers between devices  38.6 us (46%)
  blocking collectives  26.8 us (32%)
  other arithmetic  5.88 us (7%)
  matrix products  5.79 us (7%)
  local copies, waits for them, and re-layouts  3.96 us (5%)
  between operations  1.55 us (2%)
    ppermute x7, waiting for transfers between devices, on_device(): lax.ppermute(ring[-1], 'seq', [(dev, (dev + 1) % 8) for dev in range(8)])  38.6 us
    unnamed x1, blocking collectives  16.4 us
    psum x1, blocking collectives, on_device(): summed = lax.psum(columns, 'kv')  10.4 us
    dot_general x2, matrix products, block_scores(): jnp.einsum('rgid,kgd->rgik', query_block, key_block, preferred_element_ty...  5.79 us
    unnamed x21, local copies, waits for them, and re-layouts  3.82 us
    reduce_sum x1, other arithmetic, stats_block(): jnp.sum(terms, axis=-1)  3.55 us
  transfers between devices with their start and end apart: 7, of which 7 were waited for; matrix products, arithmetic and copies ran while one was open for 5% of the time, Pallas kernels for 0%

profile of v1, /device:TPU:0, one launch (start us, length us, event | category | flops | bytes accessed | tf_op | source)
XLA Modules:
  0.0 83.2 jit_solution(8823741104241487170)
XLA Ops:
  0.0 0.0 copy-start
  0.0 1.0 %copy.8 = bf16[256,2,128]{2,0,1:T(8,128)(2,1)S(1)} copy(bf16[256,2,128]{2,1,0:T(2,128)(2,1)} %param.9) | data formatting | bytes 262144 | tf_op args[2]
  1.0 0.5 collective-permute-start
  1.5 6.7 %collective-permute-done = bf16[256,2,128]{2,0,1:T(8,128)(2,1)S(1)} collective-permute-done((bf16[256,2,128]{2,0,1:T(8,128)(2,1)S(1)}, bf16[256,2,128]{2,0,1:T(8,128)(2,1)S(1)}, u32[]{:S(2)}, u32[]{:S(2)}) %collective-permute-start) | collective-permute-done | bytes 131104 | tf_op jit(solution)/shard_map/ppermute | solution.py:52
  8.2 0.0 collective-permute-start.1
  8.2 6.2 %collective-permute-done.1 = bf16[256,2,128]{2,0,1:T(8,128)(2,1)S(1)} collective-permute-done((bf16[256,2,128]{2,0,1:T(8,128)(2,1)S(1)}, bf16[256,2,128]{2,0,1:T(8,128)(2,1)S(1)}, u32[]{:S(2)}, u32[]{:S(2)}) %collective-permute-start.1) | collective-permute-done | bytes 131104 | tf_op jit(solution)/shard_map/ppermute | solution.py:52
  14.4 0.0 collective-permute-start.2
  14.4 6.2 %collective-permute-done.2 = bf16[256,2,128]{2,0,1:T(8,128)(2,1)S(1)} collective-permute-done((bf16[256,2,128]{2,0,1:T(8,128)(2,1)S(1)}, bf16[256,2,128]{2,0,1:T(8,128)(2,1)S(1)}, u32[]{:S(2)}, u32[]{:S(2)}) %collective-permute-start.2) | collective-permute-done | bytes 131104 | tf_op jit(solution)/shard_map/ppermute | solution.py:52
  20.6 0.0 collective-permute-start.3
  20.6 6.2 %collective-permute-done.3 = bf16[256,2,128]{2,0,1:T(8,128)(2,1)S(1)} collective-permute-done((bf16[256,2,128]{2,0,1:T(8,128)(2,1)S(1)}, bf16[256,2,128]{2,0,1:T(8,128)(2,1)S(1)}, u32[]{:S(2)}, u32[]{:S(2)}) %collective-permute-start.3) | collective-permute-done | bytes 131104 | tf_op jit(solution)/shard_map/ppermute | solution.py:52
  26.8 0.0 collective-permute-start.4
  26.8 6.2 %collective-permute-done.4 = bf16[256,2,128]{2,0,1:T(8,128)(2,1)S(1)} collective-permute-done((bf16[256,2,128]{2,0,1:T(8,128)(2,1)S(1)}, bf16[256,2,128]{2,0,1:T(8,128)(2,1)S(1)}, u32[]{:S(2)}, u32[]{:S(2)}) %collective-permute-start.4) | collective-permute-done | bytes 131104 | tf_op jit(solution)/shard_map/ppermute | solution.py:52
  33.0 0.0 collective-permute-start.5
  33.0 6.2 %collective-permute-done.5 = bf16[256,2,128]{2,0,1:T(8,128)(2,1)S(1)} collective-permute-done((bf16[256,2,128]{2,0,1:T(8,128)(2,1)S(1)}, bf16[256,2,128]{2,0,1:T(8,128)(2,1)S(1)}, u32[]{:S(2)}, u32[]{:S(2)}) %collective-permute-start.5) | collective-permute-done | bytes 131104 | tf_op jit(solution)/shard_map/ppermute | solution.py:52
  39.2 0.0 collective-permute-start.6
  39.2 1.4 %fusion.7 = (s32[]{:T(128)}, s32[96]{0:T(128)S(1)}) fusion(s32[768]{0:T(1024)} %param.7, s32[]{:T(128)S(6)} %select_n.28), kind=kLoop, calls=%fused_computation.31 | loop fusion | flops 95 | bytes 776 | tf_op jit(solution)/shard_map/reduce_max | solution.py:49
  41.2 1.1 %copy.11 = bf16[96,16,128]{2,0,1:T(8,128)(2,1)S(1)} copy(bf16[96,16,128]{2,1,0:T(8,128)(2,1)} %param.8) | data formatting | bytes 786432 | tf_op args[1]
  42.4 1.3 %dynamic-slice = u32[1]{0:T(128)} dynamic-slice(u32[32]{0:T(128)} %constant.86, u32[]{:T(128)S(6)} %add.58), dynamic_slice_sizes={1} | dynamic-slice | bytes 12
  44.4 1.0 %collective-permute-done.6 = bf16[256,2,128]{2,0,1:T(8,128)(2,1)S(1)} collective-permute-done((bf16[256,2,128]{2,0,1:T(8,128)(2,1)S(1)}, bf16[256,2,128]{2,0,1:T(8,128)(2,1)S(1)}, u32[]{:S(2)}, u32[]{:S(2)}) %collective-permute-start.6) | collective-permute-done | bytes 131104 | tf_op jit(solution)/shard_map/ppermute | solution.py:52
  45.5 0.0 copy-done
  45.8 0.1 constant_dynamic-slice_fusion
  45.9 6.1 %conditional.2 = ((f32[96,2,8]{0,2,1:T(8,128)S(1)}, f32[96,2,8]{0,2,1:T(8,128)S(1)})) conditional(s32[]{:T(128)} %convert_element_type.6, (f32[96,2,8]{0,2,1:T(8,128)S(1)}, f32[96,2,8]{0,2,1:T(8,128)S(1)}) %tuple.33, (s32[96]{0:T(128)S(1)}, bf16[2048,2,128]{2,0,1:T(8,128)(2,1)S(1)}, bf16[96,2,8,128]{3,0,2,1:T(8,128)(2,1)S(1)}, ...), branch_computations={%region_1.2_spmd, %region_2.5_spmd} | conditional | flops 830671872 | bytes 27277720 | solution.py:66
  45.9 0.2 iota_compare_fusion
  46.1 2.3 %fusion = (f32[96,2,8]{0,2,1:T(8,128)S(1)}, f32[2,2048,96,8]{1,2,3,0:T(8,128)S(1)}) fusion(pred[96,2048]{1,0:T(8,128)(4,1)S(1)} %iota_compare_fusion, bf16[96,2,8,128]{3,0,2,1:T(8,128)(2,1)S(1)} %get-tuple-element.91, bf16[2048,2,128]{2,0,1:T(8,128)(2,1)S(1)} %get-tuple-element.90), kind=kOutput, calls=%fused_computation.2 | convolution fusion | flops 814742016 | bytes 14227456 | tf_op jit(solution)/shard_map/while/body/eval_jaxpr/cond/branch_1_fun/rgid,kgd->rgik/dot_general | solution.py:13
  48.5 3.5 %select_reduce_fusion = f32[96,2,8]{0,2,1:T(8,128)S(1)} fusion(f32[2,2048,96,8]{1,2,3,0:T(8,128)S(1)} %get-tuple-element.110, f32[96,2,8]{0,2,1:T(8,128)S(1)} %max.2, pred[96,2048]{1,0:T(8,128)(4,1)S(1)} %iota_compare_fusion), kind=kLoop, calls=%fused_computation.1 | loop fusion | flops 15727104 | bytes 12791808 | tf_op jit(solution)/shard_map/while/body/eval_jaxpr/cond/branch_1_fun/reduce_sum | solution.py:30
  52.0 3.7 %conditional.3 = (f32[2048]{0:T(1024)S(1)}) conditional(s32[]{:T(128)} %convert_element_type.6, () %tuple.32, (s32[96]{0:T(128)S(1)}, bf16[2048,2,128]{2,0,1:T(8,128)(2,1)S(1)}, bf16[96,2,8,128]{3,0,2,1:T(8,128)(2,1)S(1)}, f32[96,2,8]{0,2,1:T(8,128)S(1)}, f32[96,2,8]{0,2,1:T(8,128)S(1)}) %tuple.50), branch_computations={%region_5.6_spmd, %region_6.8_spmd} | conditional | flops 818085376 | bytes 1868168 | solution.py:87
  52.1 0.2 iota_compare_fusion.1
  52.3 3.5 %fusion.5 = f32[2048]{0:T(1024)S(1)} fusion(f32[96,2,8]{0,2,1:T(8,128)S(1)} %add.48, pred[96,2048]{1,0:T(8,128)(4,1)S(1)} %iota_compare_fusion.1, bf16[96,2,8,128]{3,0,2,1:T(8,128)(2,1)S(1)} %get-tuple-element.95, bf16[2048,2,128]{2,0,1:T(8,128)(2,1)S(1)} %get-tuple-element.94), kind=kOutput, calls=%fused_computation.10 | convolution fusion | flops 817887232 | bytes 1652736 | tf_op jit(solution)/shard_map/while/body/eval_jaxpr/cond/branch_1_fun/rgid,kgd->rgik/dot_general | solution.py:13
  55.7 16.4 %all-reduce = f32[2048]{0:T(1024)S(1)} all-reduce(f32[2048]{0:T(1024)S(1)} %get-tuple-element.116), channel_id=2, replica_groups=mesh['kv'=4,'seq'=8] {'seq'}, use_global_device_ids=true, to_apply=%region_8.9.clone | all-reduce | flops 2048 | bytes 16384
  72.2 0.1 dynamic-slice.1
  72.2 10.4 %psum.7 = f32[256]{0:T(256)S(1)} all-reduce(f32[256]{0:T(256)S(1)} %dynamic-slice.1), channel_id=1, replica_groups=mesh['kv'=4,'seq'=8] {'kv'}, use_global_device_ids=true, to_apply=%region_9.10 | all-reduce | flops 256 | bytes 2048 | tf_op jit(solution)/shard_map/psum | solution.py:99
  82.6 0.6 broadcast_multiply_fusion
  (23 shorter events, 0.4 us)
Async XLA Ops:
  0.0 45.6 %copy-start = (bf16[256,2,128]{2,1,0:T(2,128)(2,1)S(1)}, bf16[256,2,128]{2,1,0:T(2,128)(2,1)}, u32[]{:S(2)}) copy-start(bf16[256,2,128]{2,1,0:T(2,128)(2,1)} %param.9) | copy-start | bytes 393220
  1.0 7.2 %collective-permute-start = (bf16[256,2,128]{2,0,1:T(8,128)(2,1)S(1)}, bf16[256,2,128]{2,0,1:T(8,128)(2,1)S(1)}, u32[]{:S(2)}, u32[]{:S(2)}) collective-permute-start(bf16[256,2,128]{2,0,1:T(8,128)(2,1)S(1)} %copy.8), channel_id=1, source_target_pairs={{0,1},{1,2},{2,3},{3,4},{4,5},{5,6},{6,7},{7,0},{8,9},{9,10},{10,1... | collective-permute-start | bytes 393224 | tf_op jit(solution)/shard_map/ppermute | solution.py:52
  8.2 6.2 %collective-permute-start.1 = (bf16[256,2,128]{2,0,1:T(8,128)(2,1)S(1)}, bf16[256,2,128]{2,0,1:T(8,128)(2,1)S(1)}, u32[]{:S(2)}, u32[]{:S(2)}) collective-permute-start(bf16[256,2,128]{2,0,1:T(8,128)(2,1)S(1)} %collective-permute-done), channel_id=1, source_target_pairs={{0,1},{1,2},{2,3},{3,4},{4,5},{5,6},{6,7},{7,0},{8,9},{9,10},{10,1... | collective-permute-start | bytes 393224 | tf_op jit(solution)/shard_map/ppermute | solution.py:52
  14.4 6.2 %collective-permute-start.2 = (bf16[256,2,128]{2,0,1:T(8,128)(2,1)S(1)}, bf16[256,2,128]{2,0,1:T(8,128)(2,1)S(1)}, u32[]{:S(2)}, u32[]{:S(2)}) collective-permute-start(bf16[256,2,128]{2,0,1:T(8,128)(2,1)S(1)} %collective-permute-done.1), channel_id=1, source_target_pairs={{0,1},{1,2},{2,3},{3,4},{4,5},{5,6},{6,7},{7,0},{8,9},{9,10},{10,1... | collective-permute-start | bytes 393224 | tf_op jit(solution)/shard_map/ppermute | solution.py:52
  20.6 6.2 %collective-permute-start.3 = (bf16[256,2,128]{2,0,1:T(8,128)(2,1)S(1)}, bf16[256,2,128]{2,0,1:T(8,128)(2,1)S(1)}, u32[]{:S(2)}, u32[]{:S(2)}) collective-permute-start(bf16[256,2,128]{2,0,1:T(8,128)(2,1)S(1)} %collective-permute-done.2), channel_id=1, source_target_pairs={{0,1},{1,2},{2,3},{3,4},{4,5},{5,6},{6,7},{7,0},{8,9},{9,10},{10,1... | collective-permute-start | bytes 393224 | tf_op jit(solution)/shard_map/ppermute | solution.py:52
  26.8 6.2 %collective-permute-start.4 = (bf16[256,2,128]{2,0,1:T(8,128)(2,1)S(1)}, bf16[256,2,128]{2,0,1:T(8,128)(2,1)S(1)}, u32[]{:S(2)}, u32[]{:S(2)}) collective-permute-start(bf16[256,2,128]{2,0,1:T(8,128)(2,1)S(1)} %collective-permute-done.3), channel_id=1, source_target_pairs={{0,1},{1,2},{2,3},{3,4},{4,5},{5,6},{6,7},{7,0},{8,9},{9,10},{10,1... | collective-permute-start | bytes 393224 | tf_op jit(solution)/shard_map/ppermute | solution.py:52
  33.0 6.2 %collective-permute-start.5 = (bf16[256,2,128]{2,0,1:T(8,128)(2,1)S(1)}, bf16[256,2,128]{2,0,1:T(8,128)(2,1)S(1)}, u32[]{:S(2)}, u32[]{:S(2)}) collective-permute-start(bf16[256,2,128]{2,0,1:T(8,128)(2,1)S(1)} %collective-permute-done.4), channel_id=1, source_target_pairs={{0,1},{1,2},{2,3},{3,4},{4,5},{5,6},{6,7},{7,0},{8,9},{9,10},{10,1... | collective-permute-start | bytes 393224 | tf_op jit(solution)/shard_map/ppermute | solution.py:52
  39.2 6.2 %collective-permute-start.6 = (bf16[256,2,128]{2,0,1:T(8,128)(2,1)S(1)}, bf16[256,2,128]{2,0,1:T(8,128)(2,1)S(1)}, u32[]{:S(2)}, u32[]{:S(2)}) collective-permute-start(bf16[256,2,128]{2,0,1:T(8,128)(2,1)S(1)} %collective-permute-done.5), channel_id=1, source_target_pairs={{0,1},{1,2},{2,3},{3,4},{4,5},{5,6},{6,7},{7,0},{8,9},{9,10},{10,1... | collective-permute-start | bytes 393224 | tf_op jit(solution)/shard_map/ppermute | solution.py:52
